TPU v7x, 512 devices: a whole 4x4x16 slice. The times are simulated.
512 devices in a mesh: lvl: 16 (over z), col: 32 (over y, x, core).
Axes of the slice: x: 4, y: 4, z: 16, core: 2. Of those that a mesh axis runs over, the one named last changes fastest.
Arguments:
- rhs: float32 [16, 1536, 128], P('lvl', 'col'), may hold values from -6 to 6
- panel: bfloat16 [16, 4, 1536, 1536], P('lvl', None, 'col'), may hold values from -0.078125 to 0.078125
- inverse_t: bfloat16 [16, 1536, 1536], P('lvl', 'col'), as said below
- pattern: int32 [16, 4, 12, 12], P('lvl'), may hold values 0 or 1
Outputs:
- sample: float32 [16, 1536, 128], P('lvl', 'col')
- solution: float32 [16, 1536, 128], P('lvl', 'col')
Inputs may be any that keep to these rules, and one draw needn't show every extreme that they name: `pattern`: 1 marks a 128 x 128 tile of a panel slot that is structurally nonzero. Each inverse_t[s] is upper triangular with a positive diagonal.
All inputs are finite; a program needn't handle non-finite values.
Results may differ from a plain program's by a relative error of at most 0.035.
Values may be sent and summed in bfloat16 or wider, within the bound.
A program may use at most 64 MiB of HBM per device.

v0:
```python
import jax
import jax.numpy as jnp
from jax import lax
from jax.sharding import PartitionSpec as P


def as_sent(x):

    def short(part):
        return part.astype(jnp.bfloat16) if part.dtype == jnp.float32 else part

    return jax.tree.map(short, x)


def level_rank(device_pos, levels):
    running = jnp.zeros((), jnp.int32)
    for exponent in range(1, levels + 1):
        running = running + ((device_pos + 1) % 2**exponent == 0).astype(jnp.int32)
    return running


def expand_pattern(pattern_own, row_start, row_count, full_width):
    tile_count = pattern_own.shape[1]
    tile_size = full_width // tile_count
    row_ids = row_start + lax.iota(jnp.int32, row_count)
    row_pick = (row_ids[:, None] // tile_size == lax.iota(jnp.int32, tile_count)[None, :]).astype(
        jnp.bfloat16
    )
    col_pick = (
        lax.iota(jnp.int32, full_width)[None, :] // tile_size
        == lax.iota(jnp.int32, tile_count)[:, None]
    ).astype(jnp.bfloat16)
    row_mask = jnp.einsum(
        "rb,kbc->krc",
        row_pick,
        pattern_own.astype(jnp.bfloat16),
        preferred_element_type=jnp.float32,
    ).astype(jnp.bfloat16)
    return jnp.einsum("krc,cn->krn", row_mask, col_pick, preferred_element_type=jnp.float32).astype(
        jnp.bfloat16
    )


def pick_member(everyone, member_pos, member_total):
    safe_pos = jnp.clip(member_pos, 0, member_total - 1)
    picked = lax.dynamic_index_in_dim(everyone, safe_pos, 0, keepdims=False)
    inside = jnp.logical_and(member_pos >= 0, member_pos < member_total)
    return jnp.where(inside, picked, jnp.zeros_like(picked))


def on_device(rhs, panel, inverse_t, pattern):
    member_total = lax.axis_size("lvl")
    levels = member_total.bit_length() - 1
    device_pos = lax.axis_index("lvl")
    column_pos = lax.axis_index("col")
    row_count = rhs.shape[1]
    rhs_count = rhs.shape[2]
    full_width = inverse_t.shape[2]
    height = level_rank(device_pos, levels)
    right_side = rhs[0]
    inverse_own = inverse_t[0]
    factor = panel[0] * expand_pattern(pattern[0], column_pos * row_count, row_count, full_width)
    sample = jnp.zeros((row_count, rhs_count), jnp.float32)
    upward = jnp.zeros((levels + 1, row_count, rhs_count), jnp.float32)
    for section_num in range(levels + 1):
        if section_num == 0:
            gathered = upward
        else:
            reach_dist = 2 ** (section_num - 1)
            everyone = lax.all_gather(as_sent(upward[None]), "lvl", axis=0, tiled=True)
            from_left = pick_member(everyone, device_pos - reach_dist, member_total)
            from_right = pick_member(everyone, device_pos + reach_dist, member_total)
            gathered = from_left + from_right
        active = height == section_num
        residual = (right_side - gathered[0]).astype(jnp.bfloat16)
        partial_sum = jnp.einsum(
            "ri,rn->in", inverse_own, residual, preferred_element_type=jnp.float32
        )
        solved_all = lax.psum(partial_sum.astype(jnp.bfloat16), "col").astype(jnp.float32)
        own_rows = lax.dynamic_slice_in_dim(solved_all, column_pos * row_count, row_count, 0)
        solved_half = solved_all.astype(jnp.bfloat16)
        sample = jnp.where(active, own_rows, sample)
        remain = levels - section_num
        if remain > 0:
            pushed = jnp.einsum(
                "krn,nm->krm", factor[:remain], solved_half, preferred_element_type=jnp.float32
            )
            upward = jnp.where(active, pushed + gathered[1 : remain + 1], 0.0)
    answer = jnp.zeros((row_count, rhs_count), jnp.float32)
    ancestry = jnp.zeros((levels, row_count, rhs_count), jnp.bfloat16)
    downward = ancestry
    for section_num in range(levels, -1, -1):
        remain = levels - section_num
        active = height == section_num
        if remain > 0:
            reach_dist = 2**section_num
            everyone = lax.all_gather(downward[None], "lvl", axis=0, tiled=True)
            parent_up = device_pos // (2 * reach_dist) % 2 == 0
            parent_pos = jnp.where(parent_up, device_pos + reach_dist, device_pos - reach_dist)
            received = pick_member(everyone, parent_pos, member_total)
            ancestry = ancestry.at[:remain].set(jnp.where(active, received, ancestry[:remain]))
            partial_adj = jnp.einsum(
                "krn,krm->nm",
                factor[:remain],
                ancestry[:remain],
                preferred_element_type=jnp.float32,
            )
            adjoint = lax.psum_scatter(
                partial_adj.astype(jnp.bfloat16), "col", scatter_dimension=0, tiled=True
            ).astype(jnp.float32)
            back_full = sample - adjoint
        else:
            back_full = sample
        back_whole = lax.all_gather(back_full.astype(jnp.bfloat16), "col", axis=0, tiled=True)
        solved = jnp.dot(inverse_own, back_whole, preferred_element_type=jnp.float32)
        answer = jnp.where(active, solved, answer)
        solved_half = solved.astype(jnp.bfloat16)
        if section_num > 0:
            downward = jnp.concatenate(
                [solved_half[None], ancestry[: levels - section_num]], axis=0
            )
    return (sample[None], answer[None])


def solution(mesh):
    in_specs = (
        P("lvl", "col", None),
        P("lvl", None, "col", None),
        P("lvl", "col", None),
        P("lvl", None, None, None),
    )
    out_specs = (P("lvl", "col", None), P("lvl", "col", None))
    return jax.shard_map(
        on_device, mesh=mesh, in_specs=in_specs, out_specs=out_specs, check_vma=False
    )
```

profile of v0, /device:TPU:1, one launch (start us, length us, event | category | flops | bytes accessed | tf_op | source)
XLA Modules:
  0.0 1450.9 jit_solution(16410489634673471)
XLA Ops:
  8.1 1.8 convolution_convert_fusion.6
  10.7 139.2 %all-reduce.7.cloned.1.call-done = bf16[1536,128]{1,0:T(8,128)(2,1)} async-done(((bf16[1536,128]{1,0:T(8,128)(2,1)}), bf16[1536,128]{1,0:T(8,128)(2,1)}) %all-reduce.7.cloned.1.call-update) | async-done | bytes 393232 | tf_op jit(solution)/shard_map/psum | solution.py:79
  149.9 1.3 fusion.8
  151.2 28.1 %all-gather = bf16[64,48,128]{2,1,0:T(8,128)(2,1)S(1)} all-gather(bf16[4,48,128]{2,1,0:T(8,128)(2,1)S(1)} %fusion.8), channel_id=2, replica_groups=mesh['lvl'=16,'col'=32] {'lvl'}, dimensions={0}, use_global_device_ids=true | all-gather | bytes 835584 | tf_op jit(solution)/shard_map/all_gather | solution.py:70
  180.5 136.0 %all-reduce.9.cloned.1.call-done = bf16[1536,128]{1,0:T(8,128)(2,1)} async-done(((bf16[1536,128]{1,0:T(8,128)(2,1)}), bf16[1536,128]{1,0:T(8,128)(2,1)}) %all-reduce.9.cloned.1.call-update) | async-done | bytes 393232 | tf_op jit(solution)/shard_map/psum | solution.py:79
  317.8 27.0 %all-gather.1 = bf16[48,48,128]{2,1,0:T(8,128)(2,1)S(1)} all-gather(bf16[3,48,128]{2,1,0:T(8,128)(2,1)S(1)} %fusion.10), channel_id=3, replica_groups=mesh['lvl'=16,'col'=32] {'lvl'}, dimensions={0}, use_global_device_ids=true | all-gather | bytes 626688 | tf_op jit(solution)/shard_map/all_gather | solution.py:70
  346.0 135.6 %all-reduce.11.cloned.1.call-done = bf16[1536,128]{1,0:T(8,128)(2,1)} async-done(((bf16[1536,128]{1,0:T(8,128)(2,1)}), bf16[1536,128]{1,0:T(8,128)(2,1)}) %all-reduce.11.cloned.1.call-update) | async-done | bytes 393232 | tf_op jit(solution)/shard_map/psum | solution.py:79
  482.8 26.0 %all-gather.2 = bf16[32,48,128]{2,1,0:T(8,128)(2,1)S(1)} all-gather(bf16[2,48,128]{2,1,0:T(8,128)(2,1)S(1)} %fusion.12), channel_id=4, replica_groups=mesh['lvl'=16,'col'=32] {'lvl'}, dimensions={0}, use_global_device_ids=true | all-gather | bytes 417792 | tf_op jit(solution)/shard_map/all_gather | solution.py:70
  510.0 135.7 %all-reduce.13.cloned.1.call-done = bf16[1536,128]{1,0:T(8,128)(2,1)} async-done(((bf16[1536,128]{1,0:T(8,128)(2,1)}), bf16[1536,128]{1,0:T(8,128)(2,1)}) %all-reduce.13.cloned.1.call-update) | async-done | bytes 393232 | tf_op jit(solution)/shard_map/psum | solution.py:79
  646.9 24.3 %all-gather.3 = bf16[16,48,128]{2,1,0:T(8,128)(2,1)S(1)} all-gather(bf16[1,48,128]{2,1,0:T(8,128)(2,1)S(1)} %fusion.16), channel_id=5, replica_groups=mesh['lvl'=16,'col'=32] {'lvl'}, dimensions={0}, use_global_device_ids=true | all-gather | bytes 208896 | tf_op jit(solution)/shard_map/all_gather | solution.py:70
  672.4 136.2 %all-reduce.15.cloned.1.call-done = bf16[1536,128]{1,0:T(8,128)(2,1)} async-done(((bf16[1536,128]{1,0:T(8,128)(2,1)}), bf16[1536,128]{1,0:T(8,128)(2,1)}) %all-reduce.15.cloned.1.call-update) | async-done | bytes 393232 | tf_op jit(solution)/shard_map/psum | solution.py:79
  809.4 25.8 %all_gather.43 = bf16[1536,128]{1,0:T(8,128)(2,1)S(1)} all-gather(bf16[48,128]{1,0:T(8,128)(2,1)S(1)} %get-tuple-element.62), channel_id=1, replica_groups=mesh['lvl'=16,'col'=32] {'col'}, dimensions={0}, use_global_device_ids=true | all-gather | bytes 405504 | tf_op jit(solution)/shard_map/all_gather | solution.py:114
  835.5 24.6 %all-gather.4 = bf16[768,128]{1,0:T(8,128)(2,1)S(1)} all-gather(bf16[48,128]{1,0:T(8,128)(2,1)S(1)} %convert_bitcast_fusion.3), channel_id=6, replica_groups=mesh['lvl'=16,'col'=32] {'lvl'}, dimensions={0}, use_global_device_ids=true | all-gather | bytes 208896 | tf_op jit(solution)/shard_map/all_gather | solution.py:97
  861.4 96.8 %reduce-scatter.5.cloned.1.call-done = bf16[48,128]{1,0:T(8,128)(2,1)} async-done(((bf16[1536,128]{1,0:T(8,128)(2,1)}), bf16[48,128]{1,0:T(8,128)(2,1)}) %reduce-scatter.5.cloned.1.call-update) | async-done | bytes 12304 | tf_op jit(solution)/shard_map/reduce_scatter | solution.py:108
  958.8 26.6 %all_gather.45 = bf16[1536,128]{1,0:T(8,128)(2,1)S(1)} all-gather(bf16[48,128]{1,0:T(8,128)(2,1)S(1)} %subtract_convert_fusion.3), channel_id=1, replica_groups=mesh['lvl'=16,'col'=32] {'col'}, dimensions={0}, use_global_device_ids=true | all-gather | bytes 405504 | tf_op jit(solution)/shard_map/all_gather | solution.py:114
  985.6 25.8 %all-gather.5 = bf16[32,48,128]{2,1,0:T(8,128)(2,1)S(1)} all-gather(bf16[2,48,128]{2,1,0:T(8,128)(2,1)S(1)} %pad_maximum_fusion.2), channel_id=7, replica_groups=mesh['lvl'=16,'col'=32] {'lvl'}, dimensions={0}, use_global_device_ids=true | all-gather | bytes 417792 | tf_op jit(solution)/shard_map/all_gather | solution.py:97
  1012.5 97.4 %reduce-scatter.7.cloned.1.call-done = bf16[48,128]{1,0:T(8,128)(2,1)} async-done(((bf16[1536,128]{1,0:T(8,128)(2,1)}), bf16[48,128]{1,0:T(8,128)(2,1)}) %reduce-scatter.7.cloned.1.call-update) | async-done | bytes 12304 | tf_op jit(solution)/shard_map/reduce_scatter | solution.py:108
  1110.7 26.3 %all_gather.47 = bf16[1536,128]{1,0:T(8,128)(2,1)S(1)} all-gather(bf16[48,128]{1,0:T(8,128)(2,1)S(1)} %subtract_convert_fusion.2), channel_id=1, replica_groups=mesh['lvl'=16,'col'=32] {'col'}, dimensions={0}, use_global_device_ids=true | all-gather | bytes 405504 | tf_op jit(solution)/shard_map/all_gather | solution.py:114
  1137.2 26.6 %all-gather.6 = bf16[48,48,128]{2,1,0:T(8,128)(2,1)S(1)} all-gather(bf16[3,48,128]{2,1,0:T(8,128)(2,1)S(1)} %pad_maximum_fusion.1), channel_id=8, replica_groups=mesh['lvl'=16,'col'=32] {'lvl'}, dimensions={0}, use_global_device_ids=true | all-gather | bytes 626688 | tf_op jit(solution)/shard_map/all_gather | solution.py:97
  1165.1 97.6 %reduce-scatter.9.cloned.1.call-done = bf16[48,128]{1,0:T(8,128)(2,1)} async-done(((bf16[1536,128]{1,0:T(8,128)(2,1)}), bf16[48,128]{1,0:T(8,128)(2,1)}) %reduce-scatter.9.cloned.1.call-update) | async-done | bytes 12304 | tf_op jit(solution)/shard_map/reduce_scatter | solution.py:108
  1263.4 26.3 %all_gather.49 = bf16[1536,128]{1,0:T(8,128)(2,1)S(1)} all-gather(bf16[48,128]{1,0:T(8,128)(2,1)S(1)} %subtract_convert_fusion.1), channel_id=1, replica_groups=mesh['lvl'=16,'col'=32] {'col'}, dimensions={0}, use_global_device_ids=true | all-gather | bytes 405504 | tf_op jit(solution)/shard_map/all_gather | solution.py:114
  1289.9 27.8 %all-gather.7 = bf16[64,48,128]{2,1,0:T(8,128)(2,1)S(1)} all-gather(bf16[4,48,128]{2,1,0:T(8,128)(2,1)S(1)} %pad_maximum_fusion), channel_id=9, replica_groups=mesh['lvl'=16,'col'=32] {'lvl'}, dimensions={0}, use_global_device_ids=true | all-gather | bytes 835584 | tf_op jit(solution)/shard_map/all_gather | solution.py:97
  1318.9 97.7 %reduce-scatter.11.cloned.1.call-done = bf16[48,128]{1,0:T(8,128)(2,1)} async-done(((bf16[1536,128]{1,0:T(8,128)(2,1)}), bf16[48,128]{1,0:T(8,128)(2,1)}) %reduce-scatter.11.cloned.1.call-update) | async-done | bytes 12304 | tf_op jit(solution)/shard_map/reduce_scatter | solution.py:108
  1417.3 26.3 %all_gather.51 = bf16[1536,128]{1,0:T(8,128)(2,1)S(1)} all-gather(bf16[48,128]{1,0:T(8,128)(2,1)S(1)} %subtract_convert_fusion), channel_id=1, replica_groups=mesh['lvl'=16,'col'=32] {'col'}, dimensions={0}, use_global_device_ids=true | all-gather | bytes 405504 | tf_op jit(solution)/shard_map/all_gather | solution.py:114
  (67 shorter events, 19.7 us)
Async XLA Ops:
  7.2 0.9 copy-start
  7.2 2.9 copy-start.4
  7.2 2.9 copy-start.3
  7.2 142.7 %all-reduce.7.cloned.1.call-start = ((), (), s32[]{:S(2)}) async-start(), calls=%async_computation.4 | async-start | bytes 786432 | tf_op jit(solution)/shard_map/psum | solution.py:79
  9.9 306.6 %all-reduce.9.cloned.1.call-start = ((), (), s32[]{:S(2)}) async-start(), calls=%async_computation.5 | async-start | bytes 786432 | tf_op jit(solution)/shard_map/psum | solution.py:79
  10.7 168.6 %copy-start.1 = (f32[1,48,128]{2,1,0:T(8,128)S(1)}, f32[1,48,128]{2,1,0:T(8,128)}, u32[]{:S(2)}) copy-start(f32[1,48,128]{2,1,0:T(8,128)} %param.14) | copy-start | bytes 73732
  180.5 301.1 %all-reduce.11.cloned.1.call-start = ((), (), s32[]{:S(2)}) async-start(), calls=%async_computation.6 | async-start | bytes 786432 | tf_op jit(solution)/shard_map/psum | solution.py:79
  345.9 299.8 %all-reduce.13.cloned.1.call-start = ((), (), s32[]{:S(2)}) async-start(), calls=%async_computation.7 | async-start | bytes 786432 | tf_op jit(solution)/shard_map/psum | solution.py:79
  509.9 298.7 %all-reduce.15.cloned.1.call-start = ((), (), s32[]{:S(2)}) async-start(), calls=%async_computation.8 | async-start | bytes 786432 | tf_op jit(solution)/shard_map/psum | solution.py:79
  672.3 285.8 %reduce-scatter.5.cloned.1.call-start = ((), (), s32[]{:S(2)}) async-start(), calls=%async_computation.9 | async-start | bytes 405504 | tf_op jit(solution)/shard_map/reduce_scatter | solution.py:108
  809.4 607.1 %copy-start.2 = (f32[48,128]{1,0:T(8,128)}, f32[48,128]{1,0:T(8,128)S(1)}, u32[]{:S(2)}) copy-start(f32[48,128]{1,0:T(8,128)S(1)} %get-tuple-element.63) | copy-start | bytes 73732
  861.2 248.8 %reduce-scatter.7.cloned.1.call-start = ((), (), s32[]{:S(2)}) async-start(), calls=%async_computation.10 | async-start | bytes 405504 | tf_op jit(solution)/shard_map/reduce_scatter | solution.py:108
  1012.5 250.2 %reduce-scatter.9.cloned.1.call-start = ((), (), s32[]{:S(2)}) async-start(), calls=%async_computation.11 | async-start | bytes 405504 | tf_op jit(solution)/shard_map/reduce_scatter | solution.py:108
  1165.0 251.5 %reduce-scatter.11.cloned.1.call-start = ((), (), s32[]{:S(2)}) async-start(), calls=%async_computation.12 | async-start | bytes 405504 | tf_op jit(solution)/shard_map/reduce_scatter | solution.py:108
Sparse Core Ops, SparseCore 0:
  11.2 138.5 all-reduce.6
  180.6 135.8 all-reduce.8
  346.0 135.5 all-reduce.10
  510.0 135.6 all-reduce.12
  672.4 136.1 all-reduce.14
  861.3 96.7 reduce-scatter.4
  1012.6 97.3 reduce-scatter.6
  1165.2 97.4 reduce-scatter.8
  1319.0 97.5 reduce-scatter.10
where the time goes:
time: 1450 us
  waiting for transfers between devices  1070 us (74%)
  blocking collectives  341 us (24%)
  matrix products  17.7 us (1%)
    psum x5, waiting for transfers between devices, on_device(): lax.psum(partial_sum.astype(jnp.bfloat16), 'col').astype(jnp.float32)  683 us
    reduce_scatter x4, waiting for transfers between devices, on_device(): lax.psum_scatter(partial_adj.astype(jnp.bfloat16), 'col', scatter_dimensi...  389 us
    all_gather x5, blocking collectives, on_device(): lax.all_gather(back_full.astype(jnp.bfloat16), 'col', axis=0, tiled=True)  131 us
    all_gather x4, blocking collectives, on_device(): everyone = lax.all_gather(as_sent(upward[None]), 'lvl', axis=0, tiled=True)  105 us
    all_gather x4, blocking collectives, on_device(): everyone = lax.all_gather(downward[None], 'lvl', axis=0, tiled=True)  105 us
  transfers between devices with their start and end apart: 9, of which 9 were waited for; matrix products, arithmetic and copies ran while one was open for 0% of the time, Pallas kernels for 0%

commit v1 on v0

--- a/solution.py
+++ b/solution.py
@@ -76,7 +76,9 @@
         partial_sum = jnp.einsum(
             "ri,rn->in", inverse_own, residual, preferred_element_type=jnp.float32
         )
-        solved_all = lax.psum(partial_sum.astype(jnp.bfloat16), "col").astype(jnp.float32)
+        solved_all = jnp.sum(
+            lax.all_gather(partial_sum.astype(jnp.bfloat16), "col"), axis=0
+        ).astype(jnp.float32)
         own_rows = lax.dynamic_slice_in_dim(solved_all, column_pos * row_count, row_count, 0)
         solved_half = solved_all.astype(jnp.bfloat16)
         sample = jnp.where(active, own_rows, sample)

time: 1450 us -> 1270 us (0.88)
  waiting for transfers between devices: 1070 us -> 795 us
  local copies, waits for them, and re-layouts: 0.87 us -> 53.5 us
  other arithmetic: 3.79 us -> 46.7 us
    psum x5 -> x0, waiting for transfers between devices: 683 us -> none  [on_device(): lax.psum(partial_sum.astype(jnp.bfloat16), 'col').astype(jnp.float32)]
    all_gather x0 -> x5, waiting for transfers between devices: none -> 406 us  [on_device(): lax.all_gather(partial_sum.astype(jnp.bfloat16), 'col')]
    unnamed x10 -> x14, local copies, waits for them, and re-layouts: 0.86 us -> 53.1 us
    reduce_sum x0 -> x5, other arithmetic: none -> 42.9 us  [on_device(): jnp.sum(lax.all_gather(partial_sum.astype(jnp.bfloat16), 'col'), axis=0)]
where the time goes in v1:
time: 1270 us
  waiting for transfers between devices  795 us (63%)
  blocking collectives  340 us (27%)
  local copies, waits for them, and re-layouts  53.5 us (4%)
  other arithmetic  46.7 us (4%)
  matrix products  14.8 us (1%)
  between operations  14.6 us (1%)
    all_gather x5, waiting for transfers between devices, on_device(): lax.all_gather(partial_sum.astype(jnp.bfloat16), 'col')  406 us
    reduce_scatter x4, waiting for transfers between devices, on_device(): lax.psum_scatter(partial_adj.astype(jnp.bfloat16), 'col', scatter_dimensi...  389 us
    all_gather x5, blocking collectives, on_device(): lax.all_gather(back_full.astype(jnp.bfloat16), 'col', axis=0, tiled=True)  131 us
    all_gather x4, blocking collectives, on_device(): everyone = lax.all_gather(as_sent(upward[None]), 'lvl', axis=0, tiled=True)  105 us
    all_gather x4, blocking collectives, on_device(): everyone = lax.all_gather(downward[None], 'lvl', axis=0, tiled=True)  105 us
    unnamed x14, local copies, waits for them, and re-layouts  53.1 us
    reduce_sum x5, other arithmetic, on_device(): jnp.sum(lax.all_gather(partial_sum.astype(jnp.bfloat16), 'col'), axis=0)  42.9 us
  transfers between devices with their start and end apart: 9, of which 9 were waited for; matrix products, arithmetic and copies ran while one was open for 0% of the time, Pallas kernels for 0%

profile of v1, /device:TPU:1, one launch (start us, length us, event | category | flops | bytes accessed | tf_op | source)
XLA Modules:
  0.0 1266.3 jit_solution(10775292246638291432)
XLA Ops:
  12.4 82.7 %all-gather.19.cloned.1.call-done = bf16[49152,128]{1,0:T(8,128)(2,1)} async-done(((bf16[1536,128]{1,0:T(8,128)(2,1)}), bf16[49152,128]{1,0:T(8,128)(2,1)}) %all-gather.19.cloned.1.call-update) | async-done | bytes 12582928 | tf_op jit(solution)/shard_map/all_gather | solution.py:80
  102.1 27.7 %all-gather.1 = bf16[64,48,128]{2,1,0:T(8,128)(2,1)S(1)} all-gather(bf16[4,48,128]{2,1,0:T(8,128)(2,1)S(1)} %fusion.8), channel_id=3, replica_groups=mesh['lvl'=16,'col'=32] {'lvl'}, dimensions={0}, use_global_device_ids=true | all-gather | bytes 835584 | tf_op jit(solution)/shard_map/all_gather | solution.py:70
  131.0 81.2 %all-gather.21.cloned.1.call-done = bf16[49152,128]{0,1:T(8,128)(2,1)} async-done(((bf16[1536,128]{0,1:T(8,128)(2,1)}), bf16[49152,128]{0,1:T(8,128)(2,1)}) %all-gather.21.cloned.1.call-update) | async-done | bytes 12582928 | tf_op jit(solution)/shard_map/all_gather | solution.py:80
  212.2 13.0 %copy.41 = bf16[16,8,32,1536]{3,2,1,0:T(8,128)(2,1)} copy(bf16[16,8,32,1536]{3,1,2,0:T(8,128)(2,1)} %bitcast.207) | data formatting | bytes 25165824
  234.5 26.8 %all-gather.3 = bf16[48,48,128]{2,1,0:T(8,128)(2,1)S(1)} all-gather(bf16[3,48,128]{2,1,0:T(8,128)(2,1)S(1)} %fusion.10), channel_id=5, replica_groups=mesh['lvl'=16,'col'=32] {'lvl'}, dimensions={0}, use_global_device_ids=true | all-gather | bytes 626688 | tf_op jit(solution)/shard_map/all_gather | solution.py:70
  263.0 80.5 %all-gather.23.cloned.1.call-done = bf16[49152,128]{0,1:T(8,128)(2,1)} async-done(((bf16[1536,128]{0,1:T(8,128)(2,1)}), bf16[49152,128]{0,1:T(8,128)(2,1)}) %all-gather.23.cloned.1.call-update) | async-done | bytes 12582928 | tf_op jit(solution)/shard_map/all_gather | solution.py:80
  365.8 25.9 %all-gather.5 = bf16[32,48,128]{2,1,0:T(8,128)(2,1)S(1)} all-gather(bf16[2,48,128]{2,1,0:T(8,128)(2,1)S(1)} %fusion.12), channel_id=7, replica_groups=mesh['lvl'=16,'col'=32] {'lvl'}, dimensions={0}, use_global_device_ids=true | all-gather | bytes 417792 | tf_op jit(solution)/shard_map/all_gather | solution.py:70
  392.9 80.9 %all-gather.25.cloned.1.call-done = bf16[49152,128]{0,1:T(8,128)(2,1)} async-done(((bf16[1536,128]{0,1:T(8,128)(2,1)}), bf16[49152,128]{0,1:T(8,128)(2,1)}) %all-gather.25.cloned.1.call-update) | async-done | bytes 12582928 | tf_op jit(solution)/shard_map/all_gather | solution.py:80
  473.8 13.0 %copy.43 = bf16[16,8,32,1536]{3,2,1,0:T(8,128)(2,1)} copy(bf16[16,8,32,1536]{3,1,2,0:T(8,128)(2,1)} %bitcast.206) | data formatting | bytes 25165824
  496.1 24.5 %all-gather.7 = bf16[16,48,128]{2,1,0:T(8,128)(2,1)S(1)} all-gather(bf16[1,48,128]{2,1,0:T(8,128)(2,1)S(1)} %fusion.16), channel_id=9, replica_groups=mesh['lvl'=16,'col'=32] {'lvl'}, dimensions={0}, use_global_device_ids=true | all-gather | bytes 208896 | tf_op jit(solution)/shard_map/all_gather | solution.py:70
  522.5 80.4 %all-gather.27.cloned.1.call-done = bf16[49152,128]{0,1:T(8,128)(2,1)} async-done(((bf16[1536,128]{0,1:T(8,128)(2,1)}), bf16[49152,128]{0,1:T(8,128)(2,1)}) %all-gather.27.cloned.1.call-update) | async-done | bytes 12582928 | tf_op jit(solution)/shard_map/all_gather | solution.py:80
  625.1 24.6 %all_gather.83 = bf16[1536,128]{1,0:T(8,128)(2,1)S(1)} all-gather(bf16[48,128]{1,0:T(8,128)(2,1)S(1)} %get-tuple-element.64), channel_id=1, replica_groups=mesh['lvl'=16,'col'=32] {'col'}, dimensions={0}, use_global_device_ids=true | all-gather | bytes 405504 | tf_op jit(solution)/shard_map/all_gather | solution.py:116
  649.9 24.7 %all-gather.9 = bf16[768,128]{1,0:T(8,128)(2,1)S(1)} all-gather(bf16[48,128]{1,0:T(8,128)(2,1)S(1)} %convert_bitcast_fusion.3), channel_id=11, replica_groups=mesh['lvl'=16,'col'=32] {'lvl'}, dimensions={0}, use_global_device_ids=true | all-gather | bytes 208896 | tf_op jit(solution)/shard_map/all_gather | solution.py:99
  675.8 97.3 %reduce-scatter.13.cloned.1.call-done = bf16[48,128]{1,0:T(8,128)(2,1)} async-done(((bf16[1536,128]{1,0:T(8,128)(2,1)}), bf16[48,128]{1,0:T(8,128)(2,1)}) %reduce-scatter.13.cloned.1.call-update) | async-done | bytes 12304 | tf_op jit(solution)/shard_map/reduce_scatter | solution.py:110
  773.8 26.3 %all_gather.85 = bf16[1536,128]{1,0:T(8,128)(2,1)S(1)} all-gather(bf16[48,128]{1,0:T(8,128)(2,1)S(1)} %subtract_convert_fusion.3), channel_id=1, replica_groups=mesh['lvl'=16,'col'=32] {'col'}, dimensions={0}, use_global_device_ids=true | all-gather | bytes 405504 | tf_op jit(solution)/shard_map/all_gather | solution.py:116
  800.3 25.7 %all-gather.10 = bf16[32,48,128]{2,1,0:T(8,128)(2,1)S(1)} all-gather(bf16[2,48,128]{2,1,0:T(8,128)(2,1)S(1)} %pad_maximum_fusion.2), channel_id=12, replica_groups=mesh['lvl'=16,'col'=32] {'lvl'}, dimensions={0}, use_global_device_ids=true | all-gather | bytes 417792 | tf_op jit(solution)/shard_map/all_gather | solution.py:99
  827.1 97.4 %reduce-scatter.15.cloned.1.call-done = bf16[48,128]{1,0:T(8,128)(2,1)} async-done(((bf16[1536,128]{1,0:T(8,128)(2,1)}), bf16[48,128]{1,0:T(8,128)(2,1)}) %reduce-scatter.15.cloned.1.call-update) | async-done | bytes 12304 | tf_op jit(solution)/shard_map/reduce_scatter | solution.py:110
  925.2 26.8 %all_gather.87 = bf16[1536,128]{1,0:T(8,128)(2,1)S(1)} all-gather(bf16[48,128]{1,0:T(8,128)(2,1)S(1)} %subtract_convert_fusion.2), channel_id=1, replica_groups=mesh['lvl'=16,'col'=32] {'col'}, dimensions={0}, use_global_device_ids=true | all-gather | bytes 405504 | tf_op jit(solution)/shard_map/all_gather | solution.py:116
  952.2 26.6 %all-gather.11 = bf16[48,48,128]{2,1,0:T(8,128)(2,1)S(1)} all-gather(bf16[3,48,128]{2,1,0:T(8,128)(2,1)S(1)} %pad_maximum_fusion.1), channel_id=13, replica_groups=mesh['lvl'=16,'col'=32] {'lvl'}, dimensions={0}, use_global_device_ids=true | all-gather | bytes 626688 | tf_op jit(solution)/shard_map/all_gather | solution.py:99
  980.2 97.3 %reduce-scatter.17.cloned.1.call-done = bf16[48,128]{1,0:T(8,128)(2,1)} async-done(((bf16[1536,128]{1,0:T(8,128)(2,1)}), bf16[48,128]{1,0:T(8,128)(2,1)}) %reduce-scatter.17.cloned.1.call-update) | async-done | bytes 12304 | tf_op jit(solution)/shard_map/reduce_scatter | solution.py:110
  1078.3 26.6 %all_gather.89 = bf16[1536,128]{1,0:T(8,128)(2,1)S(1)} all-gather(bf16[48,128]{1,0:T(8,128)(2,1)S(1)} %subtract_convert_fusion.1), channel_id=1, replica_groups=mesh['lvl'=16,'col'=32] {'col'}, dimensions={0}, use_global_device_ids=true | all-gather | bytes 405504 | tf_op jit(solution)/shard_map/all_gather | solution.py:116
  1105.1 27.8 %all-gather.12 = bf16[64,48,128]{2,1,0:T(8,128)(2,1)S(1)} all-gather(bf16[4,48,128]{2,1,0:T(8,128)(2,1)S(1)} %pad_maximum_fusion), channel_id=14, replica_groups=mesh['lvl'=16,'col'=32] {'lvl'}, dimensions={0}, use_global_device_ids=true | all-gather | bytes 835584 | tf_op jit(solution)/shard_map/all_gather | solution.py:99
  1134.1 97.4 %reduce-scatter.19.cloned.1.call-done = bf16[48,128]{1,0:T(8,128)(2,1)} async-done(((bf16[1536,128]{1,0:T(8,128)(2,1)}), bf16[48,128]{1,0:T(8,128)(2,1)}) %reduce-scatter.19.cloned.1.call-update) | async-done | bytes 12304 | tf_op jit(solution)/shard_map/reduce_scatter | solution.py:110
  1232.2 26.6 %all_gather.91 = bf16[1536,128]{1,0:T(8,128)(2,1)S(1)} all-gather(bf16[48,128]{1,0:T(8,128)(2,1)S(1)} %subtract_convert_fusion), channel_id=1, replica_groups=mesh['lvl'=16,'col'=32] {'col'}, dimensions={0}, use_global_device_ids=true | all-gather | bytes 405504 | tf_op jit(solution)/shard_map/all_gather | solution.py:116
  (80 shorter events, 90.2 us)
Async XLA Ops:
  7.2 0.9 copy-start
  7.2 122.7 %copy-start.1 = (f32[1,48,128]{2,1,0:T(8,128)S(1)}, f32[1,48,128]{2,1,0:T(8,128)}, u32[]{:S(2)}) copy-start(f32[1,48,128]{2,1,0:T(8,128)} %param.14) | copy-start | bytes 73732
  7.2 87.9 %all-gather.19.cloned.1.call-start = ((), (), s32[]{:S(2)}) async-start(), calls=%async_computation.4 | async-start | bytes 12976128 | tf_op jit(solution)/shard_map/all_gather | solution.py:80
  9.9 202.3 %all-gather.21.cloned.1.call-start = ((), (), s32[]{:S(2)}) async-start(), calls=%async_computation.5 | async-start | bytes 12976128 | tf_op jit(solution)/shard_map/all_gather | solution.py:80
  130.9 212.6 %all-gather.23.cloned.1.call-start = ((), (), s32[]{:S(2)}) async-start(), calls=%async_computation.6 | async-start | bytes 12976128 | tf_op jit(solution)/shard_map/all_gather | solution.py:80
  262.4 211.3 %all-gather.25.cloned.1.call-start = ((), (), s32[]{:S(2)}) async-start(), calls=%async_computation.7 | async-start | bytes 12976128 | tf_op jit(solution)/shard_map/all_gather | solution.py:80
  392.8 210.1 %all-gather.27.cloned.1.call-start = ((), (), s32[]{:S(2)}) async-start(), calls=%async_computation.8 | async-start | bytes 12976128 | tf_op jit(solution)/shard_map/all_gather | solution.py:80
  521.7 251.4 %reduce-scatter.13.cloned.1.call-start = ((), (), s32[]{:S(2)}) async-start(), calls=%async_computation.9 | async-start | bytes 405504 | tf_op jit(solution)/shard_map/reduce_scatter | solution.py:110
  625.1 634.4 %copy-start.2 = (f32[48,128]{1,0:T(8,128)}, f32[48,128]{1,0:T(8,128)S(1)}, u32[]{:S(2)}) copy-start(f32[48,128]{1,0:T(8,128)S(1)} %get-tuple-element.65) | copy-start | bytes 73732
  675.7 248.8 %reduce-scatter.15.cloned.1.call-start = ((), (), s32[]{:S(2)}) async-start(), calls=%async_computation.10 | async-start | bytes 405504 | tf_op jit(solution)/shard_map/reduce_scatter | solution.py:110
  827.0 250.5 %reduce-scatter.17.cloned.1.call-start = ((), (), s32[]{:S(2)}) async-start(), calls=%async_computation.11 | async-start | bytes 405504 | tf_op jit(solution)/shard_map/reduce_scatter | solution.py:110
  980.1 251.3 %reduce-scatter.19.cloned.1.call-start = ((), (), s32[]{:S(2)}) async-start(), calls=%async_computation.12 | async-start | bytes 405504 | tf_op jit(solution)/shard_map/reduce_scatter | solution.py:110
Sparse Core Ops, SparseCore 0:
  11.1 83.9 all-gather.18
  131.1 81.0 all-gather.20
  262.5 80.9 all-gather.22
  392.9 80.8 all-gather.24
  521.8 81.0 all-gather.26
  675.8 97.2 reduce-scatter.12
  827.2 97.2 reduce-scatter.14
  980.2 97.2 reduce-scatter.16
  1134.2 97.1 reduce-scatter.18
